TPU v7x, 256 devices: a whole 4x4x8 slice. The times are simulated.
256 devices in a mesh: rep: 8 (over x, core), own: 32 (over y, z).
Axes of the slice: x: 4, y: 4, z: 8, core: 2. Of those that a mesh axis runs over, the one named last changes fastest.
Arguments:
- replica_weights: float32 [8, 64, 512, 512], P('rep', None, 'own'), may hold values from -6 to 6
- global_weights: float32 [64, 512, 512], P(None, 'own'), may hold values from -6 to 6
- momentum: float32 [96, 512, 512], P('own'), may hold values from -4 to 4
- owners: int32 [64], replicated, may hold values from 0 to 31, as said below
Outputs:
- new_weights: float32 [64, 512, 512], P(None, 'own')
- new_momentum: float32 [96, 512, 512], P('own')
Inputs may be any that keep to these rules, and one draw needn't show every extreme that they name: `owners`: no device owns more than 3 tiles, and some device owns exactly 3.
All inputs are finite; a program needn't handle non-finite values.
Results may differ from a plain program's by a relative error of at most 0.00016.
Values sent between devices are 32-bit elements; how exact they have to be, the bound alone decides.
A program may use at most 64 MiB of HBM per device.

v0:
```python
import jax
import jax.numpy as jnp
from jax import lax
from jax.sharding import PartitionSpec as P

outer_rate = 0.7
momentum_decay = 0.5


def selection(owners, own_count, slot_count):
    count = owners.shape[0]
    position = jnp.arange(count, dtype=jnp.int32)
    earlier = (owners[:, None] == owners[None, :]) & (position[None, :] < position[:, None])
    rank = jnp.sum(earlier.astype(jnp.int32), axis=1)
    slot_id = owners * slot_count + rank
    every_slot = jnp.arange(own_count * slot_count, dtype=jnp.int32)
    return (slot_id[None, :] == every_slot[:, None]).astype(jnp.float32)


def shards(replica_weights, global_weights, momentum, owners):
    own_count = lax.axis_size("own")
    rep_count = lax.axis_size("rep")
    slot_count = momentum.shape[0]
    tile_count, row_count, col_count = global_weights.shape
    slot_table = selection(owners, own_count, slot_count)
    own_index = lax.axis_index("own")
    own_slots = lax.dynamic_slice_in_dim(slot_table, own_index * slot_count, slot_count, 0)
    filled = jnp.sum(own_slots, axis=1)[:, None, None]
    difference = global_weights - replica_weights[0]
    piece_count = difference.shape[1]
    outgoing = jnp.dot(
        slot_table,
        difference.reshape(tile_count, piece_count * col_count),
        precision=lax.Precision.HIGHEST,
    )
    outgoing = outgoing.reshape(own_count * slot_count, piece_count, col_count)
    gathered = lax.all_to_all(outgoing, "own", split_axis=0, concat_axis=1, tiled=True)
    outer_grad = lax.psum(gathered, "rep") / rep_count
    new_momentum = (momentum_decay * momentum + outer_grad) * filled
    returned = lax.all_to_all(
        outer_grad + momentum_decay * new_momentum, "own", split_axis=1, concat_axis=0, tiled=True
    )
    piece_count = returned.shape[1]
    picked = jnp.dot(
        slot_table.T,
        returned.reshape(own_count * slot_count, piece_count * col_count),
        precision=lax.Precision.HIGHEST,
    )
    update = picked.reshape(tile_count, piece_count, col_count)
    new_weights = global_weights - outer_rate * update
    return (new_weights, new_momentum)


def solution(mesh):
    return jax.shard_map(
        shards,
        mesh=mesh,
        in_specs=(P("rep", None, "own", None), P(None, "own", None), P("own", None, None), P()),
        out_specs=(P(None, "own", None), P("own", None, None)),
        check_vma=False,
    )
```

profile of v0, /device:TPU:1, one launch (start us, length us, event | category | flops | bytes accessed | tf_op | source)
XLA Modules:
  0.0 295.6 jit_solution(1551482342381695741)
XLA Ops:
  7.2 0.0 all-reduce.2.cloned.1.call-start
  7.2 0.9 convert_reduce_fusion.1
  8.1 0.7 multiply_add_fusion.1
  8.8 2.7 bitcast_subtract_fusion
  11.5 2.8 fusion.3
  14.3 1.8 copy.31
  16.2 81.4 %all_to_all.33 = f32[96,16,512]{2,1,0:T(8,128)S(1)} all-to-all(f32[96,16,512]{2,1,0:T(8,128)S(1)} %copy.31), channel_id=1, replica_groups=mesh['rep'=8,'own'=32] {'own'}, dimensions={0} | all-to-all | bytes 6291456 | tf_op jit(solution)/shard_map/all_to_all | solution.py:37
  97.6 2.0 copy.32
  99.5 0.0 copy-start.1
  99.5 0.0 all-reduce.2.cloned.1.call-update
  99.6 0.1 iota_compare_fusion
  99.7 0.1 convert_reduce_fusion
  99.8 73.1 %all-reduce.2.cloned.1.call-done = f32[3,512,512]{2,1,0:T(8,128)} async-done(((f32[3,512,512]{2,1,0:T(8,128)}), f32[3,512,512]{2,1,0:T(8,128)}) %all-reduce.2.cloned.1.call-update) | async-done | bytes 3145744 | tf_op jit(solution)/shard_map/psum | solution.py:38
  172.9 0.0 copy-done.1
  172.9 4.5 %multiply_add_fusion = (f32[3,512,512]{2,1,0:T(8,128)S(1)}, f32[3,512,512]{2,1,0:T(8,128)}) fusion(f32[3,512,512]{2,1,0:T(8,128)} %all-reduce.2.cloned.1.call-done, f32[3]{0:T(128)S(1)} %convert_reduce_fusion, f32[3,512,512]{2,1,0:T(8,128)S(1)} %copy-done.1), kind=kLoop, calls=%fused_computation.3 | loop fusion | flops 4718592 | bytes 12582924 | tf_op jit(solution)/shard_map/add | solution.py:41
  177.3 2.2 copy.33
  179.5 100.4 %all_to_all.34 = f32[3,512,512]{2,0,1:T(4,128)S(1)} all-to-all(f32[3,512,512]{2,0,1:T(4,128)S(1)} %copy.33), channel_id=1, replica_groups=mesh['rep'=8,'own'=32] {'own'}, dimensions={1} | all-to-all | bytes 6291456 | tf_op jit(solution)/shard_map/all_to_all | solution.py:40
  279.9 0.0 copy-start
  279.9 1.3 copy.34
  281.2 0.3 copy-done
  281.5 4.7 %copy_subtract_fusion = f32[64,16,512]{2,0,1:T(8,128)S(1)} fusion(f32[64,16,512]{2,1,0:T(8,128)S(1)} %copy-done, s32[64]{0:T(128)S(1)} %multiply_add_fusion.1, f32[12,8,16,512]{3,2,1,0:T(8,128)S(1)} %bitcast.40), kind=kOutput, calls=%fused_computation.9 | convolution fusion | flops 605034496 | bytes 7340288 | tf_op jit(solution)/shard_map/dot_general | solution.py:44
  286.2 2.5 copy.37
Async XLA Ops:
  7.2 165.7 %all-reduce.2.cloned.1.call-start = ((), (), s32[]{:S(2)}) async-start(), calls=%async_computation.2 | async-start | bytes 6291456 | tf_op jit(solution)/shard_map/psum | solution.py:38
  99.5 73.3 %copy-start.1 = (f32[3,512,512]{2,1,0:T(8,128)S(1)}, f32[3,512,512]{2,1,0:T(8,128)}, u32[]{:S(2)}) copy-start(f32[3,512,512]{2,1,0:T(8,128)} %param.6) | copy-start | bytes 9437188
  279.9 1.6 copy-start
Sparse Core Ops, SparseCore 0:
  99.7 73.1 all-reduce.1
where the time goes:
time: 301 us; the launch traced here: 296 us
  blocking collectives  182 us (60%)
  waiting for transfers between devices  73.2 us (24%)
  between operations  14.1 us (5%)
  local copies, waits for them, and re-layouts  10.1 us (3%)
  other arithmetic  8.9 us (3%)
  matrix products  7.52 us (2%)
    all_to_all x1, blocking collectives, shards(): lax.all_to_all(outer_grad + momentum_decay * new_momentum, 'own', split_a...  100 us
    all_to_all x1, blocking collectives, shards(): lax.all_to_all(outgoing, 'own', split_axis=0, concat_axis=1, tiled=True)  81.4 us
    psum x1, waiting for transfers between devices, shards(): outer_grad = lax.psum(gathered, 'rep') / rep_count  73.1 us
  transfers between devices with their start and end apart: 1, of which 1 were waited for; matrix products, arithmetic and copies ran while one was open for 0% of the time, Pallas kernels for 0%

commit v1 on v0

v1 whole, which is shorter than its diff:
```python
import functools

import jax
import jax.numpy as jnp
from jax import lax
from jax.experimental import pallas as pl
from jax.experimental.pallas import tpu as pltpu
from jax.sharding import PartitionSpec as P

outer_rate = 0.7
momentum_decay = 0.5
SUB, LANE = 8, 128
CORES = 2
MESH = pl.DeviceIdType.MESH


def tables(owners, own_count, cap):
    count = owners.shape[0]
    position = jnp.arange(count, dtype=jnp.int32)
    earlier = (owners[:, None] == owners[None, :]) & (position[None, :] < position[:, None])
    slot_id = owners * cap + jnp.sum(earlier.astype(jnp.int32), axis=1)
    hit = slot_id[None, :] == jnp.arange(own_count * cap, dtype=jnp.int32)[:, None]
    tile_of = jnp.sum(jnp.where(hit, position[None, :] + 1, 0), axis=1)
    return slot_id, tile_of


def kernel(
    sizes, slot_ref, tile_ref, r_ref, g_ref, m_ref, w_out, m_out,
    r_mine, r_pair, g_mine, total, far_right, far_left, part_right, part_left, grad, rows_in, m_mine, packed, grad_in,
    w_piece, m_piece,
    load_sem, pair_send, pair_recv, rows_send, rows_recv, grad_send, grad_recv, ring_send, ring_recv,
    w_send, w_recv, w_pair_send, w_pair_recv, m_send, m_recv, m_pair_send, m_pair_recv,
):
    chips, owns, cap, tiles = sizes
    half = tiles // 2
    rep, own = lax.axis_index("rep"), lax.axis_index("own")
    x, core = rep // CORES, rep % CORES
    right, left, far = lax.rem(x + 1, chips), lax.rem(x + chips - 1, chips), lax.rem(x + 2, chips)
    to_right, to_left, to_pair = right * CORES + core, left * CORES + core, x * CORES + 1 - core

    def rows(c):
        return pl.ds(pl.multiple_of(c * SUB, SUB), SUB)

    def cols(q):
        return pl.ds(pl.multiple_of(q * LANE, LANE), LANE)

    order = (far, right, left, x)

    loads = []
    for i, q in enumerate(order):
        a = pltpu.make_async_copy(r_ref.at[0, :, rows(core), cols(q)], r_mine.at[i], load_sem.at[2 * i])
        b = pltpu.make_async_copy(g_ref.at[:, rows(core), cols(q)], g_mine.at[i], load_sem.at[2 * i + 1])
        a.start()
        b.start()
        loads.append((a, b))
    m_load = pltpu.make_async_copy(m_ref.at[:, :, rows(core), cols(x)], m_mine, load_sem.at[8])
    m_load.start()

    barrier = pltpu.get_barrier_semaphore()
    for other in (to_right, to_left, to_pair):
        pl.semaphore_signal(barrier, inc=1, device_id={"rep": other}, device_id_type=MESH)

    def greet(i, carry):
        pl.semaphore_signal(barrier, inc=1, device_id={"own": lax.rem(own + i, owns)}, device_id_type=MESH)
        return carry

    lax.fori_loop(1, owns, greet, 0)
    pl.semaphore_wait(barrier, owns + 2)

    pair = []
    for i, q in enumerate(order):
        copy = pltpu.make_async_remote_copy(
            src_ref=r_ref.at[0, :, rows(1 - core), cols(q)], dst_ref=r_pair.at[i],
            send_sem=pair_send.at[i], recv_sem=pair_recv.at[i], device_id={"rep": to_pair}, device_id_type=MESH,
        )
        copy.start()
        pair.append(copy)

    own_rows = pltpu.make_async_copy(
        m_ref.at[:, own, rows(core), cols(x)], rows_in.at[pl.ds(own * cap, cap)], rows_recv
    )
    own_rows.start()

    def send_rows(i, carry):
        peer = lax.rem(own + i, owns)
        pltpu.make_async_remote_copy(
            src_ref=m_ref.at[:, peer, rows(core), cols(x)], dst_ref=rows_in.at[pl.ds(own * cap, cap)],
            send_sem=rows_send, recv_sem=rows_recv, device_id={"own": peer}, device_id_type=MESH,
        ).start()
        return carry

    lax.fori_loop(1, owns, send_rows, 0)

    def ring(index, src, dst, device):
        return pltpu.make_async_remote_copy(
            src_ref=src, dst_ref=dst, send_sem=ring_send.at[index], recv_sem=ring_recv.at[index],
            device_id={"rep": device}, device_id_type=MESH,
        )

    low, high = pl.ds(0, half), pl.ds(half, half)
    steps = [
        ring(0, total.at[0, low], far_right, to_right),
        ring(1, total.at[0, high], far_left, to_left),
        ring(2, total.at[1, high], part_right.at[high], to_right),
        ring(3, total.at[2, low], part_left.at[low], to_left),
        ring(4, total.at[1, low], part_right.at[low], to_right),
        ring(5, total.at[2, high], part_left.at[high], to_left),
    ]

    for i in range(4):
        loads[i][0].wait()
        loads[i][1].wait()
        pair[i].wait_recv()
        g = g_mine[i]
        total[i] = (g - r_mine[i]) + (g - r_pair[i])
        if i == 0:
            steps[0].start()
            steps[1].start()
        elif i == 1:
            steps[2].start()
        elif i == 2:
            steps[3].start()
    steps[0].wait_recv()
    total[1, low] += far_right[...]
    steps[4].start()
    steps[1].wait_recv()
    total[2, high] += far_left[...]
    steps[5].start()
    for i in (2, 3, 4, 5):
        steps[i].wait_recv()
    scale = 1.0 / (chips * CORES)
    grad[...] = (total[3] + part_right[...] + part_left[...]) * scale

    def pack(s, carry):
        tile = tile_ref[s]
        block = grad[jnp.maximum(tile - 1, 0)]
        packed[s] = jnp.where(tile > 0, block, 0.0)
        return carry

    lax.fori_loop(0, owns * cap, pack, 0, unroll=8)
    own_grad = pltpu.make_async_copy(packed.at[pl.ds(own * cap, cap)], grad_in.at[own], grad_recv)
    own_grad.start()

    def send_grad(i, carry):
        peer = lax.rem(own + i, owns)
        pltpu.make_async_remote_copy(
            src_ref=packed.at[pl.ds(peer * cap, cap)], dst_ref=grad_in.at[own],
            send_sem=grad_send, recv_sem=grad_recv, device_id={"own": peer}, device_id_type=MESH,
        ).start()
        return carry

    lax.fori_loop(1, owns, send_grad, 0)

    def gather(piece, place, n, send, recv, pair_send, pair_recv):
        hn = n // 2

        def over(index, src, dst, device):
            return pltpu.make_async_remote_copy(
                src_ref=src, dst_ref=dst, send_sem=send.at[index], recv_sem=recv.at[index],
                device_id={"rep": device}, device_id_type=MESH,
            )

        def across(index, src, dst):
            return pltpu.make_async_remote_copy(
                src_ref=src, dst_ref=dst, send_sem=pair_send.at[index], recv_sem=pair_recv.at[index],
                device_id={"rep": to_pair}, device_id_type=MESH,
            )

        def view(q, lo):
            return place(q, core, lo, hn)

        mine = [
            over(0, piece(0, hn), view(x, 0), to_right),
            over(1, piece(hn, hn), view(x, hn), to_left),
            over(2, piece(hn, hn), view(x, hn), to_right),
            over(3, piece(0, hn), view(x, 0), to_left),
            across(0, piece(0, n), place(x, core, 0, n)),
        ]
        relays = [over(4, view(left, 0), view(left, 0), to_right), over(5, view(right, hn), view(right, hn), to_left)]
        passes = [
            across(1, view(left, 0), view(left, 0)),
            across(2, view(right, hn), view(right, hn)),
            across(3, view(left, hn), view(left, hn)),
            across(4, view(right, 0), view(right, 0)),
            across(5, view(far, 0), view(far, 0)),
            across(6, view(far, hn), view(far, hn)),
        ]

        def first():
            for copy in mine:
                copy.start()

        def second():
            for i in range(2):
                mine[i].wait_recv()
                relays[i].start()
                passes[i].start()

        def third():
            for i in range(2):
                mine[2 + i].wait_recv()
                passes[2 + i].start()
            for i in range(2):
                relays[i].wait_recv()
                passes[4 + i].start()

        def last():
            for copy in mine + relays:
                copy.wait_send()
            mine[4].wait_recv()
            for copy in passes:
                copy.wait()

        return first, second, third, last

    pltpu.make_async_copy(rows_in, rows_in, rows_recv).wait()

    def weights(k, carry):
        block = grad[k]
        moment = momentum_decay * rows_in[slot_ref[k]] + block
        w_piece[k] = g_mine[3, k] - outer_rate * (block + momentum_decay * moment)
        return carry

    lax.fori_loop(0, tiles, weights, 0, unroll=8)
    w_first, w_second, w_third, w_last = gather(
        lambda lo, n: w_piece.at[pl.ds(lo, n)], lambda q, c, lo, n: w_out.at[pl.ds(lo, n), rows(c), cols(q)], tiles,
        w_send, w_recv, w_pair_send, w_pair_recv,
    )
    w_first()
    w_copy = pltpu.make_async_copy(w_piece, w_out.at[:, rows(core), cols(x)], load_sem.at[9])
    w_copy.start()
    w_second()

    m_load.wait()
    pltpu.make_async_copy(grad_in, grad_in, grad_recv).wait()
    for c in range(cap):
        kept = jnp.where(tile_ref[own * cap + c] > 0, momentum_decay, 0.0)
        m_piece[c] = kept * m_mine[c] + grad_in[:, c]

    def m_place(q, c, lo, n):
        return m_out.at[:, pl.ds(lo, n), rows(c), cols(q)]

    m_first, m_second, m_third, m_last = gather(
        lambda lo, n: m_piece.at[:, pl.ds(lo, n)], m_place, owns, m_send, m_recv, m_pair_send, m_pair_recv
    )
    m_first()
    m_copy = pltpu.make_async_copy(m_piece, m_out.at[:, :, rows(core), cols(x)], load_sem.at[10])
    m_copy.start()
    w_third()
    m_second()
    m_third()

    w_last()
    m_last()
    w_copy.wait()
    m_copy.wait()
    for copy in pair:
        copy.wait_send()
    for copy in steps:
        copy.wait_send()
    sent = pl.ds(0, (owns - 1) * cap)
    pltpu.make_async_copy(rows_in.at[sent], rows_in.at[sent], rows_send).wait()
    pltpu.make_async_copy(packed.at[sent], packed.at[sent], grad_send).wait()


def shards(mesh, replica_weights, global_weights, momentum, owners):
    chips, owns = mesh.shape["rep"] // CORES, mesh.shape["own"]
    tiles, piece_rows, width = global_weights.shape
    cap = momentum.shape[0]
    half = tiles // 2
    slot_id, tile_of = tables(owners, owns, cap)
    momentum = momentum.reshape(cap, owns, piece_rows, width)
    f32 = jnp.float32
    dma = pltpu.SemaphoreType.DMA
    block = (SUB, LANE)
    anywhere = pl.BlockSpec(memory_space=pl.ANY)
    smem = pl.BlockSpec(memory_space=pltpu.SMEM)
    vmem = pl.BlockSpec(memory_space=pltpu.VMEM)
    new_weights, new_momentum = pl.pallas_call(
        functools.partial(kernel, (chips, owns, cap, tiles)),
        out_shape=(
            pltpu.VMEM(global_weights.shape, f32),
            pltpu.VMEM(momentum.shape, f32),
        ),
        in_specs=[smem, smem, anywhere, anywhere, anywhere],
        out_specs=(vmem, vmem),
        scratch_shapes=[
            pltpu.VMEM((4, tiles) + block, f32),
            pltpu.VMEM((4, tiles) + block, f32),
            pltpu.VMEM((4, tiles) + block, f32),
            pltpu.VMEM((4, tiles) + block, f32),
            pltpu.VMEM((half,) + block, f32),
            pltpu.VMEM((half,) + block, f32),
            pltpu.VMEM((tiles,) + block, f32),
            pltpu.VMEM((tiles,) + block, f32),
            pltpu.VMEM((tiles,) + block, f32),
            pltpu.VMEM((owns * cap,) + block, f32),
            pltpu.VMEM((cap, owns) + block, f32),
            pltpu.VMEM((owns * cap,) + block, f32),
            pltpu.VMEM((owns, cap) + block, f32),
            pltpu.VMEM((tiles,) + block, f32),
            pltpu.VMEM((cap, owns) + block, f32),
            dma((11,)), dma((4,)), dma((4,)), dma(()), dma(()), dma(()), dma(()), dma((6,)), dma((6,)),
            dma((6,)), dma((6,)), dma((7,)), dma((7,)), dma((6,)), dma((6,)), dma((7,)), dma((7,)),
        ],
        compiler_params=pltpu.CompilerParams(
            collective_id=0, has_side_effects=True, vmem_limit_bytes=40 * 1024 * 1024
        ),
    )(slot_id, tile_of, replica_weights, global_weights, momentum)
    return new_weights, new_momentum.reshape(cap, owns * piece_rows, width)


def solution(mesh):
    return jax.shard_map(
        functools.partial(shards, mesh),
        mesh=mesh,
        in_specs=(P("rep", None, "own", None), P(None, "own", None), P("own", None, None), P()),
        out_specs=(P(None, "own", None), P("own", None, None)),
        check_vma=False,
    )
```

time: 301 us -> 63.8 us (0.21); the launches traced: 296 us -> 63.6 us
  blocking collectives: 182 us -> 0 us
  waiting for transfers between devices: 73.2 us -> 0 us
  Pallas kernels: 0 us -> 53.2 us
  between operations: 14.1 us -> 0.65 us
  matrix products: 7.52 us -> 0 us
  other arithmetic: 8.9 us -> 1.67 us
    all_to_all x2 -> x0, blocking collectives: 182 us -> none  [the longest x1 100 us: shards(): lax.all_to_all(outer_grad + momentum_decay * new_momentum, 'own', split_a...]
    psum x1 -> x0, waiting for transfers between devices: 73.1 us -> none  [shards(): outer_grad = lax.psum(gathered, 'rep') / rep_count]
    pallas_call x0 -> x1, Pallas kernels: none -> 53.2 us  [shards(): pl.pallas_call(functools.partial(kernel, (chips, owns, cap, tiles)), out_...]
    dot_general x2 -> x0, matrix products: 7.52 us -> none  [the longest x1 4.67 us: shards(): jnp.dot(slot_table.T, returned.reshape(own_count * slot_count, piece_coun...]
    unnamed x5 -> x8, local copies, waits for them, and re-layouts: 2.8 us -> 8.05 us
    add x2 -> x1, other arithmetic: 5.12 us -> 0.67 us  [tables(): tile_of = jnp.sum(jnp.where(hit, position[None, :] + 1, 0), axis=1)]
    all_to_all x2 -> x0, local copies, waits for them, and re-layouts: 3.3 us -> none  [the longest x1 1.97 us: shards(): lax.all_to_all(outgoing, 'own', split_axis=0, concat_axis=1, tiled=True)]
  transfers between devices with their start and end apart: 1 -> 0, of which waited for: 1 -> 0; matrix products, arithmetic and copies ran while one was open for 0% -> 0% of each run, Pallas kernels for 0% -> 0%
where the time goes in v1:
time: 63.8 us; the launch traced here: 63.6 us
  Pallas kernels  53.2 us (83%)
  local copies, waits for them, and re-layouts  8.05 us (13%)
  other arithmetic  1.67 us (3%)
  between operations  0.65 us (1%)
    pallas_call x1, Pallas kernels, shards(): pl.pallas_call(functools.partial(kernel, (chips, owns, cap, tiles)), out_...  53.2 us
    unnamed x8, local copies, waits for them, and re-layouts  8.05 us

profile of v1, /device:TPU:1, one launch (start us, length us, event | category | flops | bytes accessed | tf_op | source)
XLA Modules:
  0.0 63.6 jit_solution(9234159510688638601)
XLA Ops:
  0.6 0.9 %convert_reduce_fusion = s32[64]{0:T(128)S(1)} fusion(s32[64]{0:T(128)} %param.7), kind=kLoop, calls=%fused_computation.2 | loop fusion | flops 20416 | bytes 512 | tf_op jit(solution)/shard_map/reduce_sum | solution.py:21
  1.5 0.7 %iota_add_fusion = (s32[64]{0:T(128)S(1)}, s32[64]{0:T(128)S(1)}) fusion(s32[64]{0:T(128)S(1)} %convert_reduce_fusion, s32[64]{0:T(128)} %param.7), kind=kLoop, calls=%fused_computation.5 | loop fusion | flops 192 | bytes 1024 | tf_op jit(solution)/shard_map/add | solution.py:23
  2.2 0.1 select_reduce_fusion.tile_ref
  2.3 0.0 copy-start
  2.3 1.9 %copy-done = f32[3,512,512]{2,1,0:T(8,128)S(1)} copy-done((f32[3,512,512]{2,1,0:T(8,128)S(1)}, f32[3,512,512]{2,1,0:T(8,128)}, u32[]{:S(2)}) %copy-start) | copy-done | bytes 3145752
  4.2 0.0 copy-start.1
  4.2 1.6 %copy-done.1 = f32[1,64,16,512]{3,2,1,0:T(8,128)S(1)} copy-done((f32[1,64,16,512]{3,2,1,0:T(8,128)S(1)}, f32[1,64,16,512]{3,2,1,0:T(8,128)}, u32[]{:S(2)}) %copy-start.1) | copy-done | bytes 2097176
  5.8 0.0 copy-start.2
  5.8 1.6 %copy-done.2 = f32[64,16,512]{2,1,0:T(8,128)S(1)} copy-done((f32[64,16,512]{2,1,0:T(8,128)S(1)}, f32[64,16,512]{2,1,0:T(8,128)}, u32[]{:S(2)}) %copy-start.2) | copy-done | bytes 2097176
  7.4 53.2 %shard_map.59 = (f32[64,16,512]{2,1,0:T(8,128)S(1)}, f32[3,32,16,512]{3,2,1,0:T(8,128)S(1)}) custom-call(s32[64]{0:T(128)S(1)} %get-tuple-element.7.slot_ref, s32[96]{0:T(128)S(1)} %select_reduce_fusion.tile_ref, f32[1,64,16,512]{3,2,1,0:T(8,128)S(1)} %copy-done.1, f32[64,16,512]{2,1,0:T(8,128)S(1)} %copy-done.2, f32[3,32,16,512]{3,2,1,0:T(8,128)S(1)} %bitcast.3), custom_call_target="tpu_custom_call" | custom-call | tf_op jit(solution)/shard_map/pallas_call | solution.py:279
  60.6 1.3 %copy.8 = f32[64,16,512]{2,1,0:T(8,128)} copy(f32[64,16,512]{2,1,0:T(8,128)S(1)} %get-tuple-element.8) | data formatting | bytes 4194304
  61.9 1.7 %copy.9 = f32[3,512,512]{2,1,0:T(8,128)} copy(f32[3,512,512]{2,1,0:T(8,128)S(1)} %bitcast.2) | data formatting | bytes 6291456
Async XLA Ops:
  2.3 1.9 %copy-start = (f32[3,512,512]{2,1,0:T(8,128)S(1)}, f32[3,512,512]{2,1,0:T(8,128)}, u32[]{:S(2)}) copy-start(f32[3,512,512]{2,1,0:T(8,128)} %param.6) | copy-start | bytes 9437188
  4.2 1.6 %copy-start.1 = (f32[1,64,16,512]{3,2,1,0:T(8,128)S(1)}, f32[1,64,16,512]{3,2,1,0:T(8,128)}, u32[]{:S(2)}) copy-start(f32[1,64,16,512]{3,2,1,0:T(8,128)} %r_ref.1) | copy-start | bytes 6291460
  5.8 1.6 %copy-start.2 = (f32[64,16,512]{2,1,0:T(8,128)S(1)}, f32[64,16,512]{2,1,0:T(8,128)}, u32[]{:S(2)}) copy-start(f32[64,16,512]{2,1,0:T(8,128)} %g_ref.1) | copy-start | bytes 6291460

commit v2 on v1

--- a/solution.py
+++ b/solution.py
@@ -14,20 +14,26 @@
 MESH = pl.DeviceIdType.MESH
 
 
-def tables(owners, own_count, cap):
-    count = owners.shape[0]
-    position = jnp.arange(count, dtype=jnp.int32)
-    earlier = (owners[:, None] == owners[None, :]) & (position[None, :] < position[:, None])
-    slot_id = owners * cap + jnp.sum(earlier.astype(jnp.int32), axis=1)
-    hit = slot_id[None, :] == jnp.arange(own_count * cap, dtype=jnp.int32)[:, None]
-    tile_of = jnp.sum(jnp.where(hit, position[None, :] + 1, 0), axis=1)
-    return slot_id, tile_of
+def tables(owners, slots):
+    cap, own_count = slots
+    count = owners.shape[1]
+    tile = lax.broadcasted_iota(jnp.int32, (count, count), 0)
+    other = lax.broadcasted_iota(jnp.int32, (count, count), 1)
+    along = jnp.broadcast_to(owners.astype(jnp.float32), (count, count))
+    down = jnp.sum(jnp.where(tile == other, along, 0.0), axis=1, keepdims=True)
+    same = jnp.where(along == down, 1.0, 0.0)
+    slot_along = cap * along[:1] + jnp.sum(jnp.where(tile < other, same, 0.0), axis=0, keepdims=True)
+    slot_down = cap * down + jnp.sum(jnp.where(other < tile, same, 0.0), axis=1, keepdims=True)
+    place = lax.broadcasted_iota(jnp.int32, (count, LANE), 1).astype(jnp.float32)
+    number = lax.broadcasted_iota(jnp.int32, (count, LANE), 0).astype(jnp.float32) + 1.0
+    tile_along = jnp.sum(jnp.where(place == slot_down, number, 0.0), axis=0, keepdims=True)
+    return slot_along, tile_along
 
 
 def kernel(
-    sizes, slot_ref, tile_ref, r_ref, g_ref, m_ref, w_out, m_out,
+    sizes, owners_ref, r_ref, g_ref, m_ref, w_out, m_out,
     r_mine, r_pair, g_mine, total, far_right, far_left, part_right, part_left, grad, rows_in, m_mine, packed, grad_in,
-    w_piece, m_piece,
+    w_piece, m_piece, table, slots,
     load_sem, pair_send, pair_recv, rows_send, rows_recv, grad_send, grad_recv, ring_send, ring_recv,
     w_send, w_recv, w_pair_send, w_pair_recv, m_send, m_recv, m_pair_send, m_pair_recv,
 ):
@@ -106,6 +112,12 @@
         ring(4, total.at[1, low], part_right.at[low], to_right),
         ring(5, total.at[2, high], part_left.at[high], to_left),
     ]
+
+    slot_along, tile_along = tables(owners_ref[...], (cap, owns))
+    table[0:1, 0:tiles] = slot_along.astype(jnp.int32)
+    table[1:2, :] = tile_along.astype(jnp.int32)
+    table_copy = pltpu.make_async_copy(table, slots, load_sem.at[11])
+    table_copy.start()
 
     for i in range(4):
         loads[i][0].wait()
@@ -131,9 +143,11 @@
     scale = 1.0 / (chips * CORES)
     grad[...] = (total[3] + part_right[...] + part_left[...]) * scale
 
+    table_copy.wait()
+
     def pack(s, carry):
-        tile = tile_ref[s]
-        block = grad[jnp.maximum(tile - 1, 0)]
+        tile = slots[1, s]
+        block = grad[jnp.clip(tile - 1, 0, tiles - 1)]
         packed[s] = jnp.where(tile > 0, block, 0.0)
         return carry
 
@@ -217,7 +231,7 @@
 
     def weights(k, carry):
         block = grad[k]
-        moment = momentum_decay * rows_in[slot_ref[k]] + block
+        moment = momentum_decay * rows_in[jnp.clip(slots[0, k], 0, owns * cap - 1)] + block
         w_piece[k] = g_mine[3, k] - outer_rate * (block + momentum_decay * moment)
         return carry
 
@@ -234,7 +248,7 @@
     m_load.wait()
     pltpu.make_async_copy(grad_in, grad_in, grad_recv).wait()
     for c in range(cap):
-        kept = jnp.where(tile_ref[own * cap + c] > 0, momentum_decay, 0.0)
+        kept = jnp.where(slots[1, own * cap + c] > 0, momentum_decay, 0.0)
         m_piece[c] = kept * m_mine[c] + grad_in[:, c]
 
     def m_place(q, c, lo, n):
@@ -268,13 +282,12 @@
     tiles, piece_rows, width = global_weights.shape
     cap = momentum.shape[0]
     half = tiles // 2
-    slot_id, tile_of = tables(owners, owns, cap)
     momentum = momentum.reshape(cap, owns, piece_rows, width)
     f32 = jnp.float32
     dma = pltpu.SemaphoreType.DMA
     block = (SUB, LANE)
-    anywhere = pl.BlockSpec(memory_space=pl.ANY)
-    smem = pl.BlockSpec(memory_space=pltpu.SMEM)
+    space = pltpu.MemorySpace.HBM
+    hbm = pl.BlockSpec(memory_space=space)
     vmem = pl.BlockSpec(memory_space=pltpu.VMEM)
     new_weights, new_momentum = pl.pallas_call(
         functools.partial(kernel, (chips, owns, cap, tiles)),
@@ -282,7 +295,7 @@
             pltpu.VMEM(global_weights.shape, f32),
             pltpu.VMEM(momentum.shape, f32),
         ),
-        in_specs=[smem, smem, anywhere, anywhere, anywhere],
+        in_specs=[vmem, hbm, hbm, hbm],
         out_specs=(vmem, vmem),
         scratch_shapes=[
             pltpu.VMEM((4, tiles) + block, f32),
@@ -300,13 +313,18 @@
             pltpu.VMEM((owns, cap) + block, f32),
             pltpu.VMEM((tiles,) + block, f32),
             pltpu.VMEM((cap, owns) + block, f32),
-            dma((11,)), dma((4,)), dma((4,)), dma(()), dma(()), dma(()), dma(()), dma((6,)), dma((6,)),
+            pltpu.VMEM((SUB, LANE), jnp.int32),
+            pltpu.SMEM((SUB, LANE), jnp.int32),
+            dma((12,)), dma((4,)), dma((4,)), dma(()), dma(()), dma(()), dma(()), dma((6,)), dma((6,)),
             dma((6,)), dma((6,)), dma((7,)), dma((7,)), dma((6,)), dma((6,)), dma((7,)), dma((7,)),
         ],
         compiler_params=pltpu.CompilerParams(
-            collective_id=0, has_side_effects=True, vmem_limit_bytes=40 * 1024 * 1024
+            collective_id=0, has_side_effects=True, vmem_limit_bytes=57 * 1024 * 1024
         ),
-    )(slot_id, tile_of, replica_weights, global_weights, momentum)
+    )(
+        owners.reshape(1, tiles),
+        *(pltpu.with_memory_space_constraint(a, space) for a in (replica_weights, global_weights, momentum)),
+    )
     return new_weights, new_momentum.reshape(cap, owns * piece_rows, width)
 
 

time: 63.8 us -> 57.1 us (0.89)
  local copies, waits for them, and re-layouts: 8.05 us -> 2.99 us
  other arithmetic: 1.67 us -> 0 us
    unnamed x8 -> x2, local copies, waits for them, and re-layouts: 8.05 us -> 2.99 us
    reduce_sum x2 -> x0, other arithmetic: 1.01 us -> none  [the longest x1 0.91 us: tables(): slot_id = owners * cap + jnp.sum(earlier.astype(jnp.int32), axis=1)]
    add x1 -> x0, other arithmetic: 0.67 us -> none  [tables(): tile_of = jnp.sum(jnp.where(hit, position[None, :] + 1, 0), axis=1)]
where the time goes in v2:
time: 57.1 us; the launch traced here: 57 us
  Pallas kernels  53.4 us (94%)
  local copies, waits for them, and re-layouts  2.99 us (5%)
  between operations  0.64 us (1%)
    pallas_call x1, Pallas kernels, shards(): pl.pallas_call(functools.partial(kernel, (chips, owns, cap, tiles)), out_...  53.4 us
    unnamed x2, local copies, waits for them, and re-layouts  2.99 us

profile of v2, /device:TPU:1, one launch (start us, length us, event | category | flops | bytes accessed | tf_op | source)
XLA Modules:
  0.0 57.0 jit_solution(3368339290134325771)
XLA Ops:
  0.6 53.4 %shard_map.59 = (f32[64,16,512]{2,1,0:T(8,128)S(1)}, f32[3,32,16,512]{3,2,1,0:T(8,128)S(1)}) custom-call(s32[1,64]{1,0:T(1,128)} %bitcast.5, f32[1,64,16,512]{3,2,1,0:T(8,128)} %r_ref.1, f32[64,16,512]{2,1,0:T(8,128)} %g_ref.1, f32[3,32,16,512]{3,2,1,0:T(8,128)} %bitcast.4), custom_call_target="tpu_custom_call" | custom-call | tf_op jit(solution)/shard_map/pallas_call | solution.py:292
  54.0 1.3 %copy.8 = f32[64,16,512]{2,1,0:T(8,128)} copy(f32[64,16,512]{2,1,0:T(8,128)S(1)} %get-tuple-element.6) | data formatting | bytes 4194304
  55.4 1.7 %copy.9 = f32[3,512,512]{2,1,0:T(8,128)} copy(f32[3,512,512]{2,1,0:T(8,128)S(1)} %bitcast.3) | data formatting | bytes 6291456

commit v3 on v2

--- a/solution.py
+++ b/solution.py
@@ -11,6 +11,8 @@
 momentum_decay = 0.5
 SUB, LANE = 8, 128
 CORES = 2
+LINES = 4
+DISTANCES = (0, 1, 3, 2)
 MESH = pl.DeviceIdType.MESH
 
 
@@ -152,32 +154,35 @@
         return carry
 
     lax.fori_loop(0, owns * cap, pack, 0, unroll=8)
-    own_grad = pltpu.make_async_copy(packed.at[pl.ds(own * cap, cap)], grad_in.at[own], grad_recv)
+    own_grad = pltpu.make_async_copy(packed.at[pl.ds(own * cap, cap)], grad_in.at[own], grad_recv.at[0])
     own_grad.start()
 
-    def send_grad(i, carry):
-        peer = lax.rem(own + i, owns)
-        pltpu.make_async_remote_copy(
-            src_ref=packed.at[pl.ds(peer * cap, cap)], dst_ref=grad_in.at[own],
-            send_sem=grad_send, recv_sem=grad_recv, device_id={"own": peer}, device_id_type=MESH,
-        ).start()
-        return carry
-
-    lax.fori_loop(1, owns, send_grad, 0)
-
-    def gather(piece, place, n, send, recv, pair_send, pair_recv):
+    line = owns // LINES
+    y, z = own // line, lax.rem(own, line)
+    for j in DISTANCES:
+        def send_grad(i, carry):
+            peer = lax.rem(y + j, LINES) * line + lax.rem(z + i, line)
+            pltpu.make_async_remote_copy(
+                src_ref=packed.at[pl.ds(peer * cap, cap)], dst_ref=grad_in.at[own],
+                send_sem=grad_send, recv_sem=grad_recv.at[j], device_id={"own": peer}, device_id_type=MESH,
+            ).start()
+            return carry
+
+        lax.fori_loop(1 if j == 0 else 0, line, send_grad, 0)
+
+    def gather(piece, place, n, send, recv, pair_send, pair_recv, group=0):
         hn = n // 2
 
         def over(index, src, dst, device):
             return pltpu.make_async_remote_copy(
-                src_ref=src, dst_ref=dst, send_sem=send.at[index], recv_sem=recv.at[index],
+                src_ref=src, dst_ref=dst, send_sem=send.at[6 * group + index], recv_sem=recv.at[6 * group + index],
                 device_id={"rep": device}, device_id_type=MESH,
             )
 
         def across(index, src, dst):
             return pltpu.make_async_remote_copy(
-                src_ref=src, dst_ref=dst, send_sem=pair_send.at[index], recv_sem=pair_recv.at[index],
-                device_id={"rep": to_pair}, device_id_type=MESH,
+                src_ref=src, dst_ref=dst, send_sem=pair_send.at[7 * group + index],
+                recv_sem=pair_recv.at[7 * group + index], device_id={"rep": to_pair}, device_id_type=MESH,
             )
 
         def view(q, lo):
@@ -246,26 +251,38 @@
     w_second()
 
     m_load.wait()
-    pltpu.make_async_copy(grad_in, grad_in, grad_recv).wait()
-    for c in range(cap):
-        kept = jnp.where(slots[1, own * cap + c] > 0, momentum_decay, 0.0)
-        m_piece[c] = kept * m_mine[c] + grad_in[:, c]
-
-    def m_place(q, c, lo, n):
-        return m_out.at[:, pl.ds(lo, n), rows(c), cols(q)]
-
-    m_first, m_second, m_third, m_last = gather(
-        lambda lo, n: m_piece.at[:, pl.ds(lo, n)], m_place, owns, m_send, m_recv, m_pair_send, m_pair_recv
-    )
-    m_first()
+
+    def momentum_chunk(j):
+        base = lax.rem(y + LINES - j, LINES) * line
+        chunk = pl.ds(base, line)
+        pltpu.make_async_copy(grad_in.at[chunk], grad_in.at[chunk], grad_recv.at[j]).wait()
+        for c in range(cap):
+            kept = jnp.where(slots[1, own * cap + c] > 0, momentum_decay, 0.0)
+            m_piece[c, chunk] = kept * m_mine[c, chunk] + grad_in[chunk, c]
+        return gather(
+            lambda lo, n: m_piece.at[:, pl.ds(base + lo, n)],
+            lambda q, c, lo, n: m_out.at[:, pl.ds(base + lo, n), rows(c), cols(q)],
+            line, m_send, m_recv, m_pair_send, m_pair_recv, j,
+        )
+
+    chunks = []
+    for i, j in enumerate(DISTANCES):
+        chunks.append(momentum_chunk(j))
+        chunks[i][0]()
+        if i == 2:
+            w_third()
+            chunks[0][1]()
     m_copy = pltpu.make_async_copy(m_piece, m_out.at[:, :, rows(core), cols(x)], load_sem.at[10])
     m_copy.start()
-    w_third()
-    m_second()
-    m_third()
+    for i in range(LINES):
+        if i > 0:
+            chunks[i][1]()
+            chunks[i - 1][2]()
+    chunks[LINES - 1][2]()
 
     w_last()
-    m_last()
+    for chunk in chunks:
+        chunk[3]()
     w_copy.wait()
     m_copy.wait()
     for copy in pair:
@@ -315,8 +332,9 @@
             pltpu.VMEM((cap, owns) + block, f32),
             pltpu.VMEM((SUB, LANE), jnp.int32),
             pltpu.SMEM((SUB, LANE), jnp.int32),
-            dma((12,)), dma((4,)), dma((4,)), dma(()), dma(()), dma(()), dma(()), dma((6,)), dma((6,)),
-            dma((6,)), dma((6,)), dma((7,)), dma((7,)), dma((6,)), dma((6,)), dma((7,)), dma((7,)),
+            dma((12,)), dma((4,)), dma((4,)), dma(()), dma(()), dma(()), dma((LINES,)), dma((6,)), dma((6,)),
+            dma((6,)), dma((6,)), dma((7,)), dma((7,)),
+            dma((6 * LINES,)), dma((6 * LINES,)), dma((7 * LINES,)), dma((7 * LINES,)),
         ],
         compiler_params=pltpu.CompilerParams(
             collective_id=0, has_side_effects=True, vmem_limit_bytes=57 * 1024 * 1024

time: 57.1 us -> 58.5 us (1.025)
  Pallas kernels: 53.4 us -> 54.8 us
    pallas_call x1, Pallas kernels: 53.4 us -> 54.8 us  [shards(): pl.pallas_call(functools.partial(kernel, (chips, owns, cap, tiles)), out_...]
where the time goes in v3:
time: 58.5 us; the launch traced here: 58.4 us
  Pallas kernels  54.8 us (94%)
  local copies, waits for them, and re-layouts  2.99 us (5%)
  between operations  0.64 us (1%)
    pallas_call x1, Pallas kernels, shards(): pl.pallas_call(functools.partial(kernel, (chips, owns, cap, tiles)), out_...  54.8 us
    unnamed x2, local copies, waits for them, and re-layouts  2.99 us

profile of v3, /device:TPU:1, one launch (start us, length us, event | category | flops | bytes accessed | tf_op | source)
XLA Modules:
  0.0 58.4 jit_solution(1125671574029377642)
XLA Ops:
  0.6 54.8 %shard_map.59 = (f32[64,16,512]{2,1,0:T(8,128)S(1)}, f32[3,32,16,512]{3,2,1,0:T(8,128)S(1)}) custom-call(s32[1,64]{1,0:T(1,128)} %bitcast.5, f32[1,64,16,512]{3,2,1,0:T(8,128)} %r_ref.1, f32[64,16,512]{2,1,0:T(8,128)} %g_ref.1, f32[3,32,16,512]{3,2,1,0:T(8,128)} %bitcast.4), custom_call_target="tpu_custom_call" | custom-call | tf_op jit(solution)/shard_map/pallas_call | solution.py:309
  55.4 1.3 %copy.8 = f32[64,16,512]{2,1,0:T(8,128)} copy(f32[64,16,512]{2,1,0:T(8,128)S(1)} %get-tuple-element.6) | data formatting | bytes 4194304
  56.8 1.7 %copy.9 = f32[3,512,512]{2,1,0:T(8,128)} copy(f32[3,512,512]{2,1,0:T(8,128)S(1)} %bitcast.3) | data formatting | bytes 6291456

commit v4 on v2

--- a/solution.py
+++ b/solution.py
@@ -11,6 +11,9 @@
 momentum_decay = 0.5
 SUB, LANE = 8, 128
 CORES = 2
+LINES = 4
+FAR_Y = (2, 1, 3, 0)
+FAR_Z = (4, 3, 5, 2, 6, 1, 7, 0)
 MESH = pl.DeviceIdType.MESH
 
 
@@ -87,15 +90,17 @@
     )
     own_rows.start()
 
-    def send_rows(i, carry):
-        peer = lax.rem(own + i, owns)
+    line = owns // LINES
+    y, z = own // line, lax.rem(own, line)
+    peers = [
+        lax.rem(y + dy, LINES) * line + lax.rem(z + dz, line)
+        for dz in FAR_Z for dy in FAR_Y if dy or dz
+    ]
+    for peer in peers:
         pltpu.make_async_remote_copy(
             src_ref=m_ref.at[:, peer, rows(core), cols(x)], dst_ref=rows_in.at[pl.ds(own * cap, cap)],
             send_sem=rows_send, recv_sem=rows_recv, device_id={"own": peer}, device_id_type=MESH,
         ).start()
-        return carry
-
-    lax.fori_loop(1, owns, send_rows, 0)
 
     def ring(index, src, dst, device):
         return pltpu.make_async_remote_copy(
@@ -155,15 +160,11 @@
     own_grad = pltpu.make_async_copy(packed.at[pl.ds(own * cap, cap)], grad_in.at[own], grad_recv)
     own_grad.start()
 
-    def send_grad(i, carry):
-        peer = lax.rem(own + i, owns)
+    for peer in peers:
         pltpu.make_async_remote_copy(
             src_ref=packed.at[pl.ds(peer * cap, cap)], dst_ref=grad_in.at[own],
             send_sem=grad_send, recv_sem=grad_recv, device_id={"own": peer}, device_id_type=MESH,
         ).start()
-        return carry
-
-    lax.fori_loop(1, owns, send_grad, 0)
 
     def gather(piece, place, n, send, recv, pair_send, pair_recv):
         hn = n // 2

time: 57.1 us -> 57.4 us (level)
  no operation moved by 1% of the time
where the time goes in v4:
time: 57.4 us; the launch traced here: 57.3 us
  Pallas kernels  53.7 us (94%)
  local copies, waits for them, and re-layouts  2.99 us (5%)
  between operations  0.64 us (1%)
    pallas_call x1, Pallas kernels, shards(): pl.pallas_call(functools.partial(kernel, (chips, owns, cap, tiles)), out_...  53.7 us
    unnamed x2, local copies, waits for them, and re-layouts  2.99 us

profile of v4, /device:TPU:1, one launch (start us, length us, event | category | flops | bytes accessed | tf_op | source)
XLA Modules:
  0.0 57.3 jit_solution(8499460995244107962)
XLA Ops:
  0.6 53.7 %shard_map.59 = (f32[64,16,512]{2,1,0:T(8,128)S(1)}, f32[3,32,16,512]{3,2,1,0:T(8,128)S(1)}) custom-call(s32[1,64]{1,0:T(1,128)} %bitcast.5, f32[1,64,16,512]{3,2,1,0:T(8,128)} %r_ref.1, f32[64,16,512]{2,1,0:T(8,128)} %g_ref.1, f32[3,32,16,512]{3,2,1,0:T(8,128)} %bitcast.4), custom_call_target="tpu_custom_call" | custom-call | tf_op jit(solution)/shard_map/pallas_call | solution.py:293
  54.3 1.3 %copy.8 = f32[64,16,512]{2,1,0:T(8,128)} copy(f32[64,16,512]{2,1,0:T(8,128)S(1)} %get-tuple-element.6) | data formatting | bytes 4194304
  55.6 1.7 %copy.9 = f32[3,512,512]{2,1,0:T(8,128)} copy(f32[3,512,512]{2,1,0:T(8,128)S(1)} %bitcast.3) | data formatting | bytes 6291456

commit v5 on v2

--- a/solution.py
+++ b/solution.py
@@ -71,6 +71,13 @@
         return carry
 
     lax.fori_loop(1, owns, greet, 0)
+
+    slot_along, tile_along = tables(owners_ref[...], (cap, owns))
+    table[0:1, 0:tiles] = slot_along.astype(jnp.int32)
+    table[1:2, :] = tile_along.astype(jnp.int32)
+    table_copy = pltpu.make_async_copy(table, slots, load_sem.at[11])
+    table_copy.start()
+
     pl.semaphore_wait(barrier, owns + 2)
 
     pair = []
@@ -112,12 +119,6 @@
         ring(4, total.at[1, low], part_right.at[low], to_right),
         ring(5, total.at[2, high], part_left.at[high], to_left),
     ]
-
-    slot_along, tile_along = tables(owners_ref[...], (cap, owns))
-    table[0:1, 0:tiles] = slot_along.astype(jnp.int32)
-    table[1:2, :] = tile_along.astype(jnp.int32)
-    table_copy = pltpu.make_async_copy(table, slots, load_sem.at[11])
-    table_copy.start()
 
     for i in range(4):
         loads[i][0].wait()

time: 57.1 us -> 57.1 us (level)
  no operation moved by 1% of the time
where the time goes in v5:
time: 57.1 us; the launch traced here: 57 us
  Pallas kernels  53.4 us (94%)
  local copies, waits for them, and re-layouts  2.99 us (5%)
  between operations  0.64 us (1%)
    pallas_call x1, Pallas kernels, shards(): pl.pallas_call(functools.partial(kernel, (chips, owns, cap, tiles)), out_...  53.4 us
    unnamed x2, local copies, waits for them, and re-layouts  2.99 us

profile of v5, /device:TPU:1, one launch (start us, length us, event | category | flops | bytes accessed | tf_op | source)
XLA Modules:
  0.0 57.0 jit_solution(8387788093288260881)
XLA Ops:
  0.6 53.4 %shard_map.59 = (f32[64,16,512]{2,1,0:T(8,128)S(1)}, f32[3,32,16,512]{3,2,1,0:T(8,128)S(1)}) custom-call(s32[1,64]{1,0:T(1,128)} %bitcast.5, f32[1,64,16,512]{3,2,1,0:T(8,128)} %r_ref.1, f32[64,16,512]{2,1,0:T(8,128)} %g_ref.1, f32[3,32,16,512]{3,2,1,0:T(8,128)} %bitcast.4), custom_call_target="tpu_custom_call" | custom-call | tf_op jit(solution)/shard_map/pallas_call | solution.py:293
  54.0 1.3 %copy.8 = f32[64,16,512]{2,1,0:T(8,128)} copy(f32[64,16,512]{2,1,0:T(8,128)S(1)} %get-tuple-element.6) | data formatting | bytes 4194304
  55.4 1.7 %copy.9 = f32[3,512,512]{2,1,0:T(8,128)} copy(f32[3,512,512]{2,1,0:T(8,128)S(1)} %bitcast.3) | data formatting | bytes 6291456
